TPU v7x, 32 devices: a whole 2x2x4 slice. The times are simulated.
32 devices in a mesh: groups: 2 (over y), tok: 4 (over z), lay: 2 (over x), head: 2 (over core).
Axes of the slice: x: 2, y: 2, z: 4, core: 2. Of those that a mesh axis runs over, the one named last changes fastest.
Arguments:
- keys: float32 [2, 4096, 1024], P('lay', ('groups', 'tok'), 'head'), parts along dimension 1, may hold values from -80 to 80, as said below
- values: float32 [2, 4096, 1024], P('lay', ('groups', 'tok'), 'head'), parts along dimension 1, may hold values from -24 to 24
- queries: float32 [2, 32, 8192], P('lay', 'groups', 'head'), parts along dimension 1, may hold values from -620 to 620, as said below
- start_block: float32 [4096, 256], P(('groups', 'tok')), parts along dimension 0, may hold values from -6 to 6
- lengths: int32 [32], P('groups'), parts along dimension 0, may hold values from 1 to 2048, as said below
Outputs:
- attended: float32 [2, 32, 2, 4096], P('lay', 'groups', 'head', 'tok'), parts along dimension 1
There are 2 independent parts, one for each index of `groups`. A program takes and returns all parts, laid end to end along the dimension named above; each array names one. Nothing has to cross between parts.
Inputs may be any that keep to these rules, and one draw needn't show every extreme that they name: keys lie within this range. queries lie within this range. `lengths`: the longest row covers all 2048 tokens.
All inputs are finite; a program needn't handle non-finite values.
Results may differ from a plain program's by a relative error of at most 0.0003.
Values sent between devices are 32-bit elements; how exact they have to be, the bound alone decides.
No kernel may reach another device: no remote copies, remote signals or barrier semaphores. Data moves between devices by JAX's collectives and lax.ppermute only.
A program may use at most 64 MiB of HBM per device.

v0:
```python
import math
import jax
import jax.numpy as jnp
from jax import lax
from jax.sharding import PartitionSpec as P

KVH = 8
HD = 128
QH = 64
ITERS = 2
NEG = -1e30


def joined(part, axis, combine):
    gathered = jax.tree.map(lambda a: lax.all_gather(a, axis), part)

    def take(source):
        return jax.tree.map(lambda a: lax.dynamic_index_in_dim(a, source, 0, False), gathered)

    return lax.fori_loop(
        1, lax.axis_size(axis), lambda source, state: combine(state, take(source)), take(0)
    )


def gram_of(block):
    return jnp.dot(
        block.T, block, precision=lax.Precision.HIGHEST, preferred_element_type=jnp.float32
    )


def right_solve(lower, matrix):
    return lax.linalg.triangular_solve(lower, matrix, left_side=False, lower=True, transpose_a=True)


def project(keys, basis):
    return jnp.einsum("lsc,sr->lcr", keys, basis, precision=lax.Precision.HIGHEST)


def mix_block(keys, coef):
    partial_block = jnp.einsum("lsc,lcr->sr", keys, coef, precision=lax.Precision.HIGHEST)
    return lax.psum(partial_block, ("lay", "head"))


def combine(first, second):
    top = jnp.maximum(first[0], second[0])
    scale_one = jnp.exp(first[0] - top)
    scale_two = jnp.exp(second[0] - top)
    total = first[1] * scale_one + second[1] * scale_two
    summed = first[2] * scale_one[..., None] + second[2] * scale_two[..., None]
    return (top, total, summed)


def body(keys, values, queries, start_block, lengths):
    highest = lax.Precision.HIGHEST
    lay_dev, tok_dev, kv_dev = keys.shape
    rank = start_block.shape[1]
    rows = queries.shape[1]
    local_heads = queries.shape[2] // HD
    group = QH // KVH
    kv_local = kv_dev // HD

    def finish(block):
        gram, proj = lax.psum((gram_of(block), project(keys, block)), "tok")
        lower = jnp.linalg.cholesky(gram)
        coef_new = right_solve(lower, proj.reshape(-1, rank)).reshape(proj.shape)
        return (right_solve(lower, block), coef_new)

    basis, coef = finish(start_block)
    for step in range(ITERS):
        basis, coef = finish(mix_block(keys, coef))
    quer = queries.reshape(lay_dev, rows, kv_local, group, HD)
    factor = coef.reshape(lay_dev, kv_local, HD, rank)
    reduced = jnp.einsum("lbgid,lgdr->lgibr", quer, factor, precision=highest) / math.sqrt(HD)
    reduced = reduced.reshape(lay_dev, kv_local, group * rows, rank)
    scores = jnp.einsum("tr,lgxr->tlgx", basis, reduced, precision=highest)
    position = lax.axis_index("tok") * tok_dev + jnp.arange(tok_dev, dtype=jnp.int32)
    valid = position[:, None] < lengths[None, :]
    valid = jnp.tile(valid, (1, group))[:, None, None, :]
    peak = jnp.max(jnp.where(valid, scores, NEG), axis=0)
    weight = jnp.where(valid, jnp.exp(scores - peak[None]), 0.0)
    total = jnp.sum(weight, axis=0)
    vals = values.reshape(lay_dev, tok_dev, kv_local, HD)
    summed = jnp.einsum("tlgx,ltgd->lgxd", weight, vals, precision=highest)
    peak = peak.reshape(lay_dev, local_heads, rows)
    total = total.reshape(lay_dev, local_heads, rows)
    summed = summed.reshape(lay_dev, local_heads, rows, HD)
    share = local_heads // lax.axis_size("tok")
    top, whole_total, whole_sum = joined((peak, total, summed), "tok", combine)
    result = whole_sum / whole_total[..., None]
    result = lax.dynamic_slice_in_dim(result, lax.axis_index("tok") * share, share, 1)
    result = result.transpose(0, 2, 1, 3)
    return result.reshape(lay_dev, rows, 1, share * HD)


def solution(mesh):
    return jax.shard_map(
        body,
        mesh=mesh,
        in_specs=(
            P("lay", ("groups", "tok"), "head"),
            P("lay", ("groups", "tok"), "head"),
            P("lay", "groups", "head"),
            P(("groups", "tok"), None),
            P("groups"),
        ),
        out_specs=P("lay", "groups", "head", "tok"),
        check_vma=False,
    )
```

profile of v0, /device:TPU:0, one launch (start us, length us, event | category | flops | bytes accessed | tf_op | source)
XLA Modules:
  0.0 476.8 jit_solution(16566091933869575326)
XLA Ops:
  6.5 3.0 fusion.71
  9.6 2.6 fusion.9
  12.4 46.5 %all-reduce.18.cloned.1.call-done = (f32[512,256]{1,0:T(8,128)}, f32[256,256]{0,1:T(8,128)}) async-done(((f32[512,256]{1,0:T(8,128)}, f32[256,256]{0,1:T(8,128)}), (f32[512,256]{1,0:T(8,128)}, f32[256,256]{0,1:T(8,128)})) %all-reduce.18.cloned.1.call-update) | async-done | bytes 786448 | tf_op jit(solution)/shard_map/psum | solution.py:63
  59.0 1.1 copy.45
  60.2 11.7 %cholesky.172 = f32[128,128]{1,0:T(8,128)S(1)} custom-call(f32[128,128]{1,0:T(8,128)S(1)} %cholesky.270), custom_call_target="Cholesky" | custom-call | tf_op jit(solution)/shard_map/jit(cholesky)/cholesky | solution.py:64
  71.9 9.8 %custom-call.16 = f32[1,128,128]{1,2,0:T(8,128)S(1)} custom-call(f32[1,128,128]{2,1,0:T(8,128)S(1)} %get-tuple-element.288), custom_call_target="InvertDiagBlocksLowerTriangular" | custom-call | tf_op jit(solution)/shard_map/jit(cholesky)/cholesky | solution.py:64
  82.3 11.7 %cholesky.189 = f32[128,128]{1,0:T(8,128)S(1)} custom-call(f32[128,128]{1,0:T(8,128)S(1)} %convolution_subtract_fusion.6), custom_call_target="Cholesky" | custom-call | tf_op jit(solution)/shard_map/jit(cholesky)/cholesky | solution.py:64
  94.0 0.7 compare_reduce_fusion.4
  96.2 4.5 while.28
  96.5 0.6 fusion.108
  97.1 1.4 bitcast_dynamic-update-slice_fusion.6
  98.6 0.6 fusion.108
  99.2 1.4 bitcast_dynamic-update-slice_fusion.6
  100.7 19.7 %custom-call.17 = f32[2,128,128]{1,2,0:T(8,128)S(1)} custom-call(f32[2,128,128]{2,1,0:T(8,128)S(1)} %get-tuple-element.212), custom_call_target="InvertDiagBlocksLowerTriangular" | custom-call | tf_op jit(solution)/shard_map/triangular_solve/custom-call.0 | solution.py:32
  121.8 1.9 convolution_bitcast_fusion.3
  123.8 32.6 %all-reduce.10.cloned.1.call-done = f32[512,256]{0,1:T(8,128)} async-done(((f32[512,256]{0,1:T(8,128)}), f32[512,256]{0,1:T(8,128)}) %all-reduce.10.cloned.1.call-update) | async-done | bytes 524304 | tf_op jit(solution)/shard_map/psum | solution.py:41
  156.4 3.0 convolution_bitcast_fusion.2
  159.3 1.3 fusion.72
  161.1 43.7 %all-reduce.16.cloned.1.call-done = (f32[512,256]{0,1:T(8,128)}, f32[256,256]{0,1:T(8,128)}) async-done(((f32[512,256]{0,1:T(8,128)}, f32[256,256]{0,1:T(8,128)}), (f32[512,256]{0,1:T(8,128)}, f32[256,256]{0,1:T(8,128)})) %all-reduce.16.cloned.1.call-update) | async-done | bytes 786448 | tf_op jit(solution)/shard_map/psum | solution.py:63
  204.8 1.1 copy.47
  206.0 11.7 %cholesky.206 = f32[128,128]{1,0:T(8,128)S(1)} custom-call(f32[128,128]{1,0:T(8,128)S(1)} %cholesky.273), custom_call_target="Cholesky" | custom-call | tf_op jit(solution)/shard_map/jit(cholesky)/cholesky | solution.py:64
  217.8 9.8 %custom-call.18 = f32[1,128,128]{1,2,0:T(8,128)S(1)} custom-call(f32[1,128,128]{2,1,0:T(8,128)S(1)} %get-tuple-element.284), custom_call_target="InvertDiagBlocksLowerTriangular" | custom-call | tf_op jit(solution)/shard_map/jit(cholesky)/cholesky | solution.py:64
  228.1 11.7 %cholesky.223 = f32[128,128]{1,0:T(8,128)S(1)} custom-call(f32[128,128]{1,0:T(8,128)S(1)} %convolution_subtract_fusion.5), custom_call_target="Cholesky" | custom-call | tf_op jit(solution)/shard_map/jit(cholesky)/cholesky | solution.py:64
  239.8 0.7 compare_reduce_fusion.2
  240.5 0.7 compare_reduce_fusion.3
  242.6 16.1 %while.29 = (s32[]{:T(128)}, f32[256,256]{1,0:T(8,128)S(1)}, s32[2,2]{1,0:T(2,128)S(1)}, f32[2,128,128]{2,1,0:T(8,128)S(1)}, s32[]{:T(128)}) while((s32[]{:T(128)}, f32[256,256]{1,0:T(8,128)S(1)}, s32[2,2]{1,0:T(2,128)S(1)}, f32[2,128,128]{2,1,0:T(8,128)S(1)}, s32[]{:T(128)}) %tuple.129), condition=%wide.while_cond.clone, body=%wide.while_body.clone.sunk | while | flops 2 | bytes 131181 | solution.py:32
  254.5 0.6 fusion.109
  255.1 1.4 bitcast_dynamic-update-slice_fusion.7
  256.6 0.6 fusion.109
  257.3 1.4 bitcast_dynamic-update-slice_fusion.7
  258.7 19.7 %custom-call.19 = f32[2,128,128]{1,2,0:T(8,128)S(1)} custom-call(f32[2,128,128]{2,1,0:T(8,128)S(1)} %get-tuple-element.213), custom_call_target="InvertDiagBlocksLowerTriangular" | custom-call | tf_op jit(solution)/shard_map/triangular_solve/custom-call.0 | solution.py:32
  279.7 1.9 convolution_bitcast_fusion.1
  281.6 32.6 %all-reduce.12.cloned.1.call-done = f32[512,256]{0,1:T(8,128)} async-done(((f32[512,256]{0,1:T(8,128)}), f32[512,256]{0,1:T(8,128)}) %all-reduce.12.cloned.1.call-update) | async-done | bytes 524304 | tf_op jit(solution)/shard_map/psum | solution.py:41
  314.2 3.0 convolution_bitcast_fusion
  317.2 1.3 fusion.73
  318.6 0.9 copy-done.15
  319.4 0.7 copy.73
  320.2 0.6 copy-done.16
  321.1 1.6 reshape.164
  322.7 39.9 %all-reduce.14.cloned.1.call-done = (f32[512,256]{0,1:T(8,128)}, f32[256,256]{0,1:T(8,128)}) async-done(((f32[512,256]{0,1:T(8,128)}, f32[256,256]{0,1:T(8,128)}), (f32[512,256]{0,1:T(8,128)}, f32[256,256]{0,1:T(8,128)})) %all-reduce.14.cloned.1.call-update) | async-done | bytes 786448 | tf_op jit(solution)/shard_map/psum | solution.py:63
  362.6 1.1 copy.50
  363.8 11.7 %cholesky.240 = f32[128,128]{1,0:T(8,128)S(1)} custom-call(f32[128,128]{1,0:T(8,128)S(1)} %cholesky.276), custom_call_target="Cholesky" | custom-call | tf_op jit(solution)/shard_map/jit(cholesky)/cholesky | solution.py:64
  375.6 9.8 %custom-call.20 = f32[1,128,128]{1,2,0:T(8,128)S(1)} custom-call(f32[1,128,128]{2,1,0:T(8,128)S(1)} %get-tuple-element.280), custom_call_target="InvertDiagBlocksLowerTriangular" | custom-call | tf_op jit(solution)/shard_map/jit(cholesky)/cholesky | solution.py:64
  385.9 11.7 %cholesky.257 = f32[128,128]{1,0:T(8,128)S(1)} custom-call(f32[128,128]{1,0:T(8,128)S(1)} %convolution_subtract_fusion.4), custom_call_target="Cholesky" | custom-call | tf_op jit(solution)/shard_map/jit(cholesky)/cholesky | solution.py:64
  397.6 0.7 compare_reduce_fusion
  398.4 0.7 compare_reduce_fusion.1
  400.5 4.5 while.30
  401.3 1.4 bitcast_dynamic-update-slice_fusion.8
  402.8 0.6 fusion.110
  403.5 1.4 bitcast_dynamic-update-slice_fusion.8
  404.9 19.7 %custom-call.21 = f32[2,128,128]{1,2,0:T(8,128)S(1)} custom-call(f32[2,128,128]{2,1,0:T(8,128)S(1)} %get-tuple-element.214), custom_call_target="InvertDiagBlocksLowerTriangular" | custom-call | tf_op jit(solution)/shard_map/triangular_solve/custom-call.0 | solution.py:32
  426.6 1.1 fusion.61
  429.2 1.7 convolution_multiply_fusion
  430.9 1.9 select_reduce_fusion
  432.8 2.6 fusion.11
  436.0 13.2 %all_gather.10 = f32[4,1,32,16]{2,3,1,0:T(8,128)S(1)} all-gather(f32[1,1,32,16]{2,3,1,0:T(8,128)S(1)} %copy.57), channel_id=1, replica_groups=mesh['groups'=2,'tok'=4,'lay'=2,'head'=2] {'tok'}, dimensions={0}, use_global_device_ids=true | all-gather | bytes 10240 | tf_op jit(solution)/shard_map/all_gather | solution.py:15
  449.2 13.3 %all_gather.9 = f32[4,1,32,16]{2,3,1,0:T(8,128)S(1)} all-gather(f32[1,1,32,16]{2,3,1,0:T(8,128)S(1)} %copy.56), channel_id=1, replica_groups=mesh['groups'=2,'tok'=4,'lay'=2,'head'=2] {'tok'}, dimensions={0}, use_global_device_ids=true | all-gather | bytes 10240 | tf_op jit(solution)/shard_map/all_gather | solution.py:15
  462.5 1.0 all-gather.2.cloned.1.call-done
  463.5 1.0 slice_bitcast_fusion
  464.5 4.3 while.27
  464.7 1.2 fusion.107
  466.2 1.2 fusion.107
  467.6 1.2 fusion.107
  469.0 0.7 copy.61
  (122 shorter events, 11.1 us)
Async XLA Ops:
  6.5 3.0 copy-start
  6.5 3.0 copy-start.2
  6.5 52.4 %all-reduce.18.cloned.1.call-start = ((), (), s32[]{:S(2)}) async-start(), calls=%async_computation.5 | async-start | bytes 1572864 | tf_op jit(solution)/shard_map/psum | solution.py:63
  12.2 144.2 %all-reduce.10.cloned.1.call-start = ((), (), s32[]{:S(2)}) async-start(), calls=%async_computation | async-start | bytes 1048576 | tf_op jit(solution)/shard_map/psum | solution.py:41
  59.0 1.2 copy-start.6
  96.1 24.3 %copy-start.13 = (f32[512,256]{1,0:T(8,128)S(1)}, f32[512,256]{1,0:T(8,128)}, u32[]{:S(2)}) copy-start(f32[512,256]{1,0:T(8,128)} %get-tuple-element.265) | copy-start | bytes 1572868
  123.7 81.1 %all-reduce.16.cloned.1.call-start = ((), (), s32[]{:S(2)}) async-start(), calls=%async_computation.4 | async-start | bytes 1572864 | tf_op jit(solution)/shard_map/psum | solution.py:63
  156.4 3.0 copy-start.3
  160.7 153.5 %all-reduce.12.cloned.1.call-start = ((), (), s32[]{:S(2)}) async-start(), calls=%async_computation.1 | async-start | bytes 1048576 | tf_op jit(solution)/shard_map/psum | solution.py:41
  204.8 1.2 copy-start.7
  242.6 35.8 %copy-start.14 = (f32[512,256]{0,1:T(8,128)S(1)}, f32[512,256]{0,1:T(8,128)}, u32[]{:S(2)}) copy-start(f32[512,256]{0,1:T(8,128)} %get-tuple-element.263) | copy-start | bytes 1572868
  281.5 81.0 %all-reduce.14.cloned.1.call-start = ((), (), s32[]{:S(2)}) async-start(), calls=%async_computation.3 | async-start | bytes 1572864 | tf_op jit(solution)/shard_map/psum | solution.py:63
  314.2 3.0 copy-start.1
  318.5 0.9 copy-start.15
  318.5 145.0 %all-gather.2.cloned.1.call-start = ((), (), s32[]{:S(2)}) async-start(), calls=%async_computation.2 | async-start | bytes 1310720 | tf_op jit(solution)/shard_map/all_gather | solution.py:15
  320.2 0.7 copy-start.16
  362.6 1.2 copy-start.4
  363.8 11.7 %copy-start.8 = (f32[256,256]{1,0:T(8,128)}, f32[256,256]{1,0:T(8,128)S(1)}, u32[]{:S(2)}) copy-start(f32[256,256]{1,0:T(8,128)S(1)} %fusion.34) | copy-start | bytes 786436
  375.6 9.8 %copy-start.9 = (f32[256,256]{1,0:T(8,128)S(1)}, f32[256,256]{1,0:T(8,128)}, u32[]{:S(2)}) copy-start(f32[256,256]{1,0:T(8,128)} %copy-done.8) | copy-start | bytes 786436
  424.6 0.6 copy-start.10
  425.7 0.9 copy-start.11
  425.7 2.0 copy-start.12
  429.2 1.7 copy-start.5
Sparse Core Ops, SparseCore 0:
  12.3 46.5 all-reduce.17
  123.8 32.5 all-reduce.9
  160.8 43.8 all-reduce.15
  281.7 32.4 all-reduce.11
  318.6 43.8 all-reduce.13
  435.6 27.8 all-gather.1
where the time goes:
time: 480 us; the launch traced here: 477 us
  waiting for transfers between devices  196 us (41%)
  other arithmetic  167 us (35%)
  matrix products  31.4 us (7%)
  blocking collectives  26.5 us (6%)
  local copies, waits for them, and re-layouts  24 us (5%)
  between operations  18.3 us (4%)
  loops' own time  12.5 us (3%)
    psum x3, waiting for transfers between devices, finish(): gram, proj = lax.psum((gram_of(block), project(keys, block)), 'tok')  130 us
    another operation x20, other arithmetic, finish(): lower = jnp.linalg.cholesky(gram)  103 us
    psum x2, waiting for transfers between devices, mix_block(): return lax.psum(partial_block, ('lay', 'head'))  65.2 us
    another operation x8, other arithmetic, right_solve(): lax.linalg.triangular_solve(lower, matrix, left_side=False, lower=True, t...  59.2 us
    all_gather x2, blocking collectives, joined(): gathered = jax.tree.map(lambda a: lax.all_gather(a, axis), part)  26.5 us
    another operation x22, local copies, waits for them, and re-layouts, right_solve(): lax.linalg.triangular_solve(lower, matrix, left_side=False, lower=True, t...  12.7 us
    another operation x3, loops' own time, right_solve(): lax.linalg.triangular_solve(lower, matrix, left_side=False, lower=True, t...  12.4 us
  transfers between devices with their start and end apart: 6, of which 6 were waited for; matrix products, arithmetic and copies ran while one was open for 1% of the time, Pallas kernels for 0%

commit v1 on v0

--- a/solution.py
+++ b/solution.py
@@ -38,7 +38,7 @@
 
 def mix_block(keys, coef):
     partial_block = jnp.einsum("lsc,lcr->sr", keys, coef, precision=lax.Precision.HIGHEST)
-    return lax.psum(partial_block, ("lay", "head"))
+    return jnp.sum(lax.all_gather(partial_block, ("lay", "head")), axis=0)
 
 
 def combine(first, second):

time: 480 us -> 464 us (0.967)
  waiting for transfers between devices: 196 us -> 176 us
  loops' own time: 12.5 us -> 0.93 us
  other arithmetic: 167 us -> 175 us
    psum x2 -> x0, waiting for transfers between devices: 65.2 us -> none  [mix_block(): return lax.psum(partial_block, ('lay', 'head'))]
    all_gather x0 -> x2, waiting for transfers between devices: none -> 44.1 us  [mix_block(): return jnp.sum(lax.all_gather(partial_block, ('lay', 'head')), axis=0)]
    another operation x3, loops' own time: 12.4 us -> 0.79 us  [right_solve(): lax.linalg.triangular_solve(lower, matrix, left_side=False, lower=True, t...]
    all_gather x0 -> x2, local copies, waits for them, and re-layouts: none -> 6.31 us  [mix_block(): return jnp.sum(lax.all_gather(partial_block, ('lay', 'head')), axis=0)]
    reduce_sum x0 -> x2, other arithmetic: none -> 4.96 us  [mix_block(): return jnp.sum(lax.all_gather(partial_block, ('lay', 'head')), axis=0)]
    another operation x22 -> x23, local copies, waits for them, and re-layouts: 12.7 us -> 12.2 us  [right_solve(): lax.linalg.triangular_solve(lower, matrix, left_side=False, lower=True, t...]
where the time goes in v1:
time: 464 us; the launch traced here: 460 us
  waiting for transfers between devices  176 us (38%)
  other arithmetic  175 us (38%)
  matrix products  35.1 us (8%)
  local copies, waits for them, and re-layouts  28.7 us (6%)
  blocking collectives  26.5 us (6%)
  between operations  18 us (4%)
    psum x3, waiting for transfers between devices, finish(): gram, proj = lax.psum((gram_of(block), project(keys, block)), 'tok')  130 us
    another operation x20, other arithmetic, finish(): lower = jnp.linalg.cholesky(gram)  103 us
    another operation x8, other arithmetic, right_solve(): lax.linalg.triangular_solve(lower, matrix, left_side=False, lower=True, t...  59.2 us
    all_gather x2, waiting for transfers between devices, mix_block(): return jnp.sum(lax.all_gather(partial_block, ('lay', 'head')), axis=0)  44.1 us
    all_gather x2, blocking collectives, joined(): gathered = jax.tree.map(lambda a: lax.all_gather(a, axis), part)  26.5 us
    another operation x23, local copies, waits for them, and re-layouts, right_solve(): lax.linalg.triangular_solve(lower, matrix, left_side=False, lower=True, t...  12.2 us
  transfers between devices with their start and end apart: 6, of which 6 were waited for; matrix products, arithmetic and copies ran while one was open for 1% of the time, Pallas kernels for 0%

profile of v1, /device:TPU:0, one launch (start us, length us, event | category | flops | bytes accessed | tf_op | source)
XLA Modules:
  0.0 460.3 jit_solution(3311239385310967649)
XLA Ops:
  6.5 3.0 fusion.71
  9.5 3.7 fusion.9
  13.5 46.5 %all-reduce.12.cloned.1.call-done = (f32[512,256]{1,0:T(8,128)}, f32[256,256]{0,1:T(8,128)}) async-done(((f32[512,256]{1,0:T(8,128)}, f32[256,256]{0,1:T(8,128)}), (f32[512,256]{1,0:T(8,128)}, f32[256,256]{0,1:T(8,128)})) %all-reduce.12.cloned.1.call-update) | async-done | bytes 786448 | tf_op jit(solution)/shard_map/psum | solution.py:63
  60.0 1.1 copy.45
  61.1 1.0 fusion.36
  62.1 11.7 %cholesky.172 = f32[128,128]{1,0:T(8,128)S(1)} custom-call(f32[128,128]{1,0:T(8,128)S(1)} %cholesky.270), custom_call_target="Cholesky" | custom-call | tf_op jit(solution)/shard_map/jit(cholesky)/cholesky | solution.py:64
  73.9 9.8 %custom-call.16 = f32[1,128,128]{1,2,0:T(8,128)S(1)} custom-call(f32[1,128,128]{2,1,0:T(8,128)S(1)} %get-tuple-element.288), custom_call_target="InvertDiagBlocksLowerTriangular" | custom-call | tf_op jit(solution)/shard_map/jit(cholesky)/cholesky | solution.py:64
  84.2 11.7 %cholesky.189 = f32[128,128]{1,0:T(8,128)S(1)} custom-call(f32[128,128]{1,0:T(8,128)S(1)} %convolution_subtract_fusion.6), custom_call_target="Cholesky" | custom-call | tf_op jit(solution)/shard_map/jit(cholesky)/cholesky | solution.py:64
  96.0 0.7 compare_reduce_fusion.4
  98.1 4.3 while.28
  99.0 1.3 bitcast_dynamic-update-slice_fusion.6
  101.0 1.3 bitcast_dynamic-update-slice_fusion.6
  102.4 19.7 %custom-call.17 = f32[2,128,128]{1,2,0:T(8,128)S(1)} custom-call(f32[2,128,128]{2,1,0:T(8,128)S(1)} %get-tuple-element.212), custom_call_target="InvertDiagBlocksLowerTriangular" | custom-call | tf_op jit(solution)/shard_map/triangular_solve/custom-call.0 | solution.py:32
  123.5 1.9 convolution_bitcast_fusion.3
  125.4 22.0 %all-gather.8.cloned.1.call-done = f32[2048,256]{0,1:T(8,128)} async-done(((f32[512,256]{0,1:T(8,128)}), f32[2048,256]{0,1:T(8,128)}) %all-gather.8.cloned.1.call-update) | async-done | bytes 2097168 | tf_op jit(solution)/shard_map/all_gather | solution.py:41
  147.5 2.7 reshape.203
  150.1 2.1 reduce_sum.27
  152.3 3.0 convolution_bitcast_fusion.2
  155.3 1.3 fusion.72
  157.1 43.6 %all-reduce.10.cloned.1.call-done = (f32[512,256]{0,1:T(8,128)}, f32[256,256]{0,1:T(8,128)}) async-done(((f32[512,256]{0,1:T(8,128)}, f32[256,256]{0,1:T(8,128)}), (f32[512,256]{0,1:T(8,128)}, f32[256,256]{0,1:T(8,128)})) %all-reduce.10.cloned.1.call-update) | async-done | bytes 786448 | tf_op jit(solution)/shard_map/psum | solution.py:63
  200.7 1.1 copy.47
  201.8 1.0 fusion.35
  202.8 11.7 %cholesky.206 = f32[128,128]{1,0:T(8,128)S(1)} custom-call(f32[128,128]{1,0:T(8,128)S(1)} %cholesky.273), custom_call_target="Cholesky" | custom-call | tf_op jit(solution)/shard_map/jit(cholesky)/cholesky | solution.py:64
  214.6 9.8 %custom-call.18 = f32[1,128,128]{1,2,0:T(8,128)S(1)} custom-call(f32[1,128,128]{2,1,0:T(8,128)S(1)} %get-tuple-element.284), custom_call_target="InvertDiagBlocksLowerTriangular" | custom-call | tf_op jit(solution)/shard_map/jit(cholesky)/cholesky | solution.py:64
  224.9 11.7 %cholesky.223 = f32[128,128]{1,0:T(8,128)S(1)} custom-call(f32[128,128]{1,0:T(8,128)S(1)} %convolution_subtract_fusion.5), custom_call_target="Cholesky" | custom-call | tf_op jit(solution)/shard_map/jit(cholesky)/cholesky | solution.py:64
  237.3 0.7 compare_reduce_fusion.3
  239.3 4.3 while.29
  240.2 1.3 bitcast_dynamic-update-slice_fusion.7
  242.2 1.3 bitcast_dynamic-update-slice_fusion.7
  243.6 19.7 %custom-call.19 = f32[2,128,128]{1,2,0:T(8,128)S(1)} custom-call(f32[2,128,128]{2,1,0:T(8,128)S(1)} %get-tuple-element.213), custom_call_target="InvertDiagBlocksLowerTriangular" | custom-call | tf_op jit(solution)/shard_map/triangular_solve/custom-call.0 | solution.py:32
  264.5 1.9 convolution_bitcast_fusion.1
  266.4 22.0 %all-gather.10.cloned.1.call-done = f32[2048,256]{0,1:T(8,128)} async-done(((f32[512,256]{0,1:T(8,128)}), f32[2048,256]{0,1:T(8,128)}) %all-gather.10.cloned.1.call-update) | async-done | bytes 2097168 | tf_op jit(solution)/shard_map/all_gather | solution.py:41
  288.5 3.6 reshape.204
  292.1 2.8 reduce_sum.28
  295.0 1.9 convolution_bitcast_fusion
  296.8 1.3 fusion.73
  298.5 0.8 copy.73
  299.5 1.6 reshape.164
  301.1 0.9 copy.72
  302.0 40.3 %all-reduce.8.cloned.1.call-done = (f32[512,256]{0,1:T(8,128)}, f32[256,256]{0,1:T(8,128)}) async-done(((f32[512,256]{0,1:T(8,128)}, f32[256,256]{0,1:T(8,128)}), (f32[512,256]{0,1:T(8,128)}, f32[256,256]{0,1:T(8,128)})) %all-reduce.8.cloned.1.call-update) | async-done | bytes 786448 | tf_op jit(solution)/shard_map/psum | solution.py:63
  342.2 1.1 copy.50
  343.3 1.0 fusion.34
  344.3 11.7 %cholesky.240 = f32[128,128]{1,0:T(8,128)S(1)} custom-call(f32[128,128]{1,0:T(8,128)S(1)} %cholesky.276), custom_call_target="Cholesky" | custom-call | tf_op jit(solution)/shard_map/jit(cholesky)/cholesky | solution.py:64
  356.1 9.8 %custom-call.20 = f32[1,128,128]{1,2,0:T(8,128)S(1)} custom-call(f32[1,128,128]{2,1,0:T(8,128)S(1)} %get-tuple-element.280), custom_call_target="InvertDiagBlocksLowerTriangular" | custom-call | tf_op jit(solution)/shard_map/jit(cholesky)/cholesky | solution.py:64
  366.4 11.7 %cholesky.257 = f32[128,128]{1,0:T(8,128)S(1)} custom-call(f32[128,128]{1,0:T(8,128)S(1)} %convolution_subtract_fusion.4), custom_call_target="Cholesky" | custom-call | tf_op jit(solution)/shard_map/jit(cholesky)/cholesky | solution.py:64
  378.8 0.7 compare_reduce_fusion.1
  380.8 4.3 while.30
  381.8 1.3 bitcast_dynamic-update-slice_fusion.8
  383.8 1.3 bitcast_dynamic-update-slice_fusion.8
  385.2 19.7 %custom-call.21 = f32[2,128,128]{1,2,0:T(8,128)S(1)} custom-call(f32[2,128,128]{2,1,0:T(8,128)S(1)} %get-tuple-element.214), custom_call_target="InvertDiagBlocksLowerTriangular" | custom-call | tf_op jit(solution)/shard_map/triangular_solve/custom-call.0 | solution.py:32
  405.9 1.6 convolution_subtract_fusion.1
  407.5 2.0 fusion.61
  409.5 1.3 fusion.26
  411.8 1.7 convolution_multiply_fusion
  413.5 2.8 select_reduce_fusion
  416.3 2.7 fusion.11
  419.5 13.2 %all_gather.26 = f32[4,1,32,16]{2,3,1,0:T(8,128)S(1)} all-gather(f32[1,1,32,16]{2,3,1,0:T(8,128)S(1)} %copy.57), channel_id=1, replica_groups=mesh['groups'=2,'tok'=4,'lay'=2,'head'=2] {'tok'}, dimensions={0}, use_global_device_ids=true | all-gather | bytes 10240 | tf_op jit(solution)/shard_map/all_gather | solution.py:15
  432.7 13.3 %all_gather.25 = f32[4,1,32,16]{2,3,1,0:T(8,128)S(1)} all-gather(f32[1,1,32,16]{2,3,1,0:T(8,128)S(1)} %copy.56), channel_id=1, replica_groups=mesh['groups'=2,'tok'=4,'lay'=2,'head'=2] {'tok'}, dimensions={0}, use_global_device_ids=true | all-gather | bytes 10240 | tf_op jit(solution)/shard_map/all_gather | solution.py:15
  446.0 1.0 all-gather.6.cloned.1.call-done
  447.1 1.0 slice_bitcast_fusion
  448.0 4.3 while.27
  448.3 1.2 fusion.107
  449.7 1.2 fusion.107
  451.2 1.2 fusion.107
  (112 shorter events, 15.2 us)
Async XLA Ops:
  6.5 3.0 copy-start
  6.5 53.4 %all-reduce.12.cloned.1.call-start = ((), (), s32[]{:S(2)}) async-start(), calls=%async_computation.5 | async-start | bytes 1572864 | tf_op jit(solution)/shard_map/psum | solution.py:63
  13.2 134.2 %all-gather.8.cloned.1.call-start = ((), (), s32[]{:S(2)}) async-start(), calls=%async_computation.1 | async-start | bytes 2621440 | tf_op jit(solution)/shard_map/all_gather | solution.py:41
  60.0 62.1 %copy-start.5 = (f32[512,256]{1,0:T(8,128)S(1)}, f32[512,256]{1,0:T(8,128)}, u32[]{:S(2)}) copy-start(f32[512,256]{1,0:T(8,128)} %get-tuple-element.265) | copy-start | bytes 1572868
  125.4 75.3 %all-reduce.10.cloned.1.call-start = ((), (), s32[]{:S(2)}) async-start(), calls=%async_computation.4 | async-start | bytes 1572864 | tf_op jit(solution)/shard_map/psum | solution.py:63
  152.3 3.0 copy-start.1
  156.6 131.9 %all-gather.10.cloned.1.call-start = ((), (), s32[]{:S(2)}) async-start(), calls=%async_computation.2 | async-start | bytes 2621440 | tf_op jit(solution)/shard_map/all_gather | solution.py:41
  200.7 62.6 %copy-start.6 = (f32[512,256]{0,1:T(8,128)S(1)}, f32[512,256]{0,1:T(8,128)}, u32[]{:S(2)}) copy-start(f32[512,256]{0,1:T(8,128)} %get-tuple-element.263) | copy-start | bytes 1572868
  266.4 75.8 %all-reduce.8.cloned.1.call-start = ((), (), s32[]{:S(2)}) async-start(), calls=%async_computation.3 | async-start | bytes 1572864 | tf_op jit(solution)/shard_map/psum | solution.py:63
  295.0 3.5 copy-start.7
  295.0 4.3 copy-start.8
  298.2 148.9 %all-gather.6.cloned.1.call-start = ((), (), s32[]{:S(2)}) async-start(), calls=%async_computation | async-start | bytes 1310720 | tf_op jit(solution)/shard_map/all_gather | solution.py:15
  404.9 0.7 copy-start.2
  405.5 4.0 copy-start.4
  405.9 5.2 %copy-start.3 = (f32[2,128,128]{1,2,0:T(8,128)S(1)}, f32[2,128,128]{1,2,0:T(8,128)}, u32[]{:S(2)}) copy-start(f32[2,128,128]{1,2,0:T(8,128)} %copy-done.2) | copy-start | bytes 393220
Sparse Core Ops, SparseCore 0:
  13.4 46.5 all-reduce.11
  125.5 21.9 all-gather.7
  156.7 43.8 all-reduce.9
  266.5 21.9 all-gather.9
  298.3 43.8 all-reduce.7
  419.2 27.8 all-gather.5
